TPU v7x, 32 devices: a whole 2x2x4 slice. The times are simulated.
32 devices in a mesh: fsdp: 4 (over z), col: 8 (over y, x, core).
Axes of the slice: x: 2, y: 2, z: 4, core: 2. Of those that a mesh axis runs over, the one named last changes fastest.
Arguments:
- grad: float32 [8192, 28672], P(('fsdp', 'col')), may hold values from -40 to 40
- basis_old: float32 [8192, 512], P(('fsdp', 'col')), may hold values from -0.0625 to 0.0625
- moment: float32 [512, 28672], P('fsdp', 'col'), may hold values from -6 to 6
Outputs:
- lowrank_grad: float32 [512, 28672], P('fsdp', 'col')
- new_moment: float32 [512, 28672], P('fsdp', 'col')
All inputs are finite; a program needn't handle non-finite values.
Results may differ from a plain program's by a relative error of at most 0.017.
Values may be sent and summed in bfloat16 or wider, within the bound.
No kernel may reach another device: no remote copies, remote signals or barrier semaphores. Data moves between devices by JAX's collectives and lax.ppermute only.
A program may use at most 128 MiB of HBM per device.

v0:
```python
import jax
import jax.numpy as jnp
from jax import lax
from jax.sharding import PartitionSpec as P

R = 512
ITERS = 2
NS_STEPS = 5
schulz_a = 3.4445
schulz_b = -4.775
schulz_c = 2.0315


def orthogonal_sharded(image):
    highest = lax.Precision.HIGHEST
    scale = lax.psum(jnp.sum(image * image), ("fsdp", "col"))
    ortho = image / jnp.sqrt(scale)
    for schulz_step in range(NS_STEPS):
        gram = lax.psum(jnp.dot(ortho.T, ortho, precision=highest), ("fsdp", "col"))
        poly = schulz_b * gram + schulz_c * jnp.dot(gram, gram, precision=highest)
        ortho = schulz_a * ortho + jnp.dot(ortho, poly, precision=highest)
    return ortho


def local(grad, basis_old, moment):
    highest = lax.Precision.HIGHEST
    grad_tile = lax.all_to_all(
        grad.astype(jnp.bfloat16), "col", split_axis=1, concat_axis=0, tiled=True
    )
    basis = basis_old
    for iteration in range(ITERS):
        basis_half = basis.astype(jnp.bfloat16)
        partial_coeff = lax.dot_general(
            grad_tile,
            lax.all_gather(basis_half, "col", axis=0, tiled=True),
            (((0,), (0,)), ((), ())),
            preferred_element_type=jnp.float32,
        )
        coeff = lax.psum(partial_coeff.astype(jnp.bfloat16), "fsdp")
        image = lax.psum_scatter(
            jnp.dot(grad_tile, coeff, preferred_element_type=jnp.float32).astype(jnp.bfloat16),
            "col",
            scatter_dimension=0,
            tiled=True,
        ).astype(jnp.float32)
        basis = orthogonal_sharded(image)
    gathered = lax.all_gather(basis.astype(jnp.bfloat16), "col", axis=0, tiled=True)
    share = R // lax.axis_size("fsdp")
    lowrank_grad = lax.psum_scatter(
        lax.dot_general(
            gathered, grad_tile, (((0,), (0,)), ((), ())), preferred_element_type=jnp.float32
        ).astype(jnp.bfloat16),
        "fsdp",
        scatter_dimension=0,
        tiled=True,
    ).astype(jnp.float32)
    margin = lax.psum(jnp.dot(basis.T, basis_old, precision=highest), ("fsdp", "col"))
    own_block = lax.axis_index("fsdp")
    margin_rows = lax.dynamic_slice_in_dim(margin, own_block * share, share, 0)
    new_moment = jnp.zeros((share, moment.shape[1]), jnp.float32) + jnp.dot(
        margin_rows,
        lax.all_gather(moment.astype(jnp.bfloat16), "fsdp", axis=0, tiled=True).astype(jnp.float32),
        precision=highest,
    )
    return (lowrank_grad, new_moment)


def solution(mesh):
    placed = (P(("fsdp", "col"), None), P(("fsdp", "col"), None), P("fsdp", "col"))
    return jax.shard_map(
        local,
        mesh=mesh,
        in_specs=placed,
        out_specs=(P("fsdp", "col"), P("fsdp", "col")),
        check_vma=False,
    )
```

profile of v0, /device:TPU:0, one launch (start us, length us, event | category | flops | bytes accessed | tf_op | source)
XLA Modules:
  0.0 2444.1 jit_solution(9534226656882063459)
XLA Ops:
  7.2 23.0 copy.23
  30.2 5.7 all-to-all-start
  36.7 169.7 %all-to-all-done = bf16[256,8,3584]{0,2,1:T(8,128)(2,1)} async-done(((bf16[256,8,3584]{0,2,1:T(8,128)(2,1)}), bf16[256,8,3584]{0,2,1:T(8,128)(2,1)}, u32[]{:S(2)}, u32[]{:S(2)}) %all-to-all-start) | async-done | bytes 14680096 | tf_op jit(solution)/shard_map/all_to_all | solution.py:27
  206.5 18.8 copy.24
  225.2 13.0 convolution_convert_fusion.2
  238.3 138.3 %all-reduce.14.cloned.1.call-done = bf16[3584,512]{1,0:T(8,128)(2,1)} async-done(((bf16[3584,512]{1,0:T(8,128)(2,1)}), bf16[3584,512]{1,0:T(8,128)(2,1)}) %all-reduce.14.cloned.1.call-update) | async-done | bytes 3670032 | tf_op jit(solution)/shard_map/psum | solution.py:39
  376.5 13.2 fusion.1
  389.8 40.2 %reduce-scatter.4.cloned.1.call-done = bf16[256,512]{0,1:T(8,128)(2,1)} async-done(((bf16[2048,512]{0,1:T(8,128)(2,1)}), bf16[256,512]{0,1:T(8,128)(2,1)}) %reduce-scatter.4.cloned.1.call-update) | async-done | bytes 262160 | tf_op jit(solution)/shard_map/reduce_scatter | solution.py:40
  430.1 1.8 fusion.14
  431.8 39.5 %psum.106 = f32[]{:T(128)} all-reduce(f32[]{:T(128)} %fusion.14), channel_id=1, replica_groups=mesh['fsdp'=4,'col'=8] {'fsdp','col'}, use_global_device_ids=true, to_apply=%region_3.0 | all-reduce | flops 1 | bytes 8 | tf_op jit(solution)/shard_map/psum | solution.py:16
  472.0 3.1 fusion.16
  475.7 131.2 %all-reduce.16.cloned.1.call-done = f32[512,512]{1,0:T(8,128)} async-done(((f32[512,512]{1,0:T(8,128)}), f32[512,512]{1,0:T(8,128)}) %all-reduce.16.cloned.1.call-update) | async-done | bytes 1048592 | tf_op jit(solution)/shard_map/psum | solution.py:19
  606.9 3.8 fusion.12
  610.8 1.8 convolution_add_fusion.9
  612.6 2.0 fusion.26
  614.7 129.7 %all-reduce.18.cloned.1.call-done = f32[512,512]{1,0:T(8,128)} async-done(((f32[512,512]{1,0:T(8,128)}), f32[512,512]{1,0:T(8,128)}) %all-reduce.18.cloned.1.call-update) | async-done | bytes 1048592 | tf_op jit(solution)/shard_map/psum | solution.py:19
  744.4 3.8 fusion.11
  748.3 1.8 convolution_add_fusion.8
  750.1 2.0 fusion.27
  752.3 129.6 %all-reduce.20.cloned.1.call-done = f32[512,512]{1,0:T(8,128)} async-done(((f32[512,512]{1,0:T(8,128)}), f32[512,512]{1,0:T(8,128)}) %all-reduce.20.cloned.1.call-update) | async-done | bytes 1048592 | tf_op jit(solution)/shard_map/psum | solution.py:19
  881.9 3.8 fusion.10
  885.8 1.8 convolution_add_fusion.7
  887.6 2.0 fusion.28
  889.7 129.7 %all-reduce.22.cloned.1.call-done = f32[512,512]{1,0:T(8,128)} async-done(((f32[512,512]{1,0:T(8,128)}), f32[512,512]{1,0:T(8,128)}) %all-reduce.22.cloned.1.call-update) | async-done | bytes 1048592 | tf_op jit(solution)/shard_map/psum | solution.py:19
  1019.4 3.8 fusion.9
  1023.3 1.8 convolution_add_fusion.6
  1025.1 2.0 fusion.29
  1027.4 129.5 %all-reduce.24.cloned.1.call-done = f32[512,512]{1,0:T(8,128)} async-done(((f32[512,512]{1,0:T(8,128)}), f32[512,512]{1,0:T(8,128)}) %all-reduce.24.cloned.1.call-update) | async-done | bytes 1048592 | tf_op jit(solution)/shard_map/psum | solution.py:19
  1156.9 3.8 fusion.8
  1160.8 2.5 fusion.13
  1163.4 27.2 %all-gather.7.cloned.1.call-done = bf16[2048,512]{0,1:T(8,128)(2,1)} async-done(((bf16[256,512]{0,1:T(8,128)(2,1)}), bf16[2048,512]{0,1:T(8,128)(2,1)}) %all-gather.7.cloned.1.call-update) | async-done | bytes 2097168 | tf_op jit(solution)/shard_map/all_gather | solution.py:35
  1190.5 12.9 fusion
  1203.5 138.1 %all-reduce.26.cloned.1.call-done = bf16[3584,512]{0,1:T(8,128)(2,1)} async-done(((bf16[3584,512]{0,1:T(8,128)(2,1)}), bf16[3584,512]{0,1:T(8,128)(2,1)}) %all-reduce.26.cloned.1.call-update) | async-done | bytes 3670032 | tf_op jit(solution)/shard_map/psum | solution.py:39
  1341.6 13.1 fusion.2
  1354.8 40.2 %reduce-scatter.6.cloned.1.call-done = bf16[256,512]{0,1:T(8,128)(2,1)} async-done(((bf16[2048,512]{0,1:T(8,128)(2,1)}), bf16[256,512]{0,1:T(8,128)(2,1)}) %reduce-scatter.6.cloned.1.call-update) | async-done | bytes 262160 | tf_op jit(solution)/shard_map/reduce_scatter | solution.py:40
  1396.8 39.5 %psum.113 = f32[]{:T(128)} all-reduce(f32[]{:T(128)} %fusion.15), channel_id=1, replica_groups=mesh['fsdp'=4,'col'=8] {'fsdp','col'}, use_global_device_ids=true, to_apply=%region_12.0 | all-reduce | flops 1 | bytes 8 | tf_op jit(solution)/shard_map/psum | solution.py:16
  1437.0 3.1 fusion.17
  1440.6 131.3 %all-reduce.28.cloned.1.call-done = f32[512,512]{1,0:T(8,128)} async-done(((f32[512,512]{1,0:T(8,128)}), f32[512,512]{1,0:T(8,128)}) %all-reduce.28.cloned.1.call-update) | async-done | bytes 1048592 | tf_op jit(solution)/shard_map/psum | solution.py:19
  1572.0 3.8 fusion.7
  1575.8 1.8 convolution_add_fusion.4
  1577.6 2.0 fusion.30
  1579.7 129.7 %all-reduce.30.cloned.1.call-done = f32[512,512]{1,0:T(8,128)} async-done(((f32[512,512]{1,0:T(8,128)}), f32[512,512]{1,0:T(8,128)}) %all-reduce.30.cloned.1.call-update) | async-done | bytes 1048592 | tf_op jit(solution)/shard_map/psum | solution.py:19
  1709.5 3.8 fusion.6
  1713.3 1.8 convolution_add_fusion.3
  1715.1 2.0 fusion.31
  1717.4 129.6 %all-reduce.32.cloned.1.call-done = f32[512,512]{1,0:T(8,128)} async-done(((f32[512,512]{1,0:T(8,128)}), f32[512,512]{1,0:T(8,128)}) %all-reduce.32.cloned.1.call-update) | async-done | bytes 1048592 | tf_op jit(solution)/shard_map/psum | solution.py:19
  1847.0 3.8 fusion.5
  1850.8 1.8 convolution_add_fusion.2
  1852.6 2.0 fusion.32
  1854.7 129.7 %all-reduce.34.cloned.1.call-done = f32[512,512]{1,0:T(8,128)} async-done(((f32[512,512]{1,0:T(8,128)}), f32[512,512]{1,0:T(8,128)}) %all-reduce.34.cloned.1.call-update) | async-done | bytes 1048592 | tf_op jit(solution)/shard_map/psum | solution.py:19
  1984.5 3.8 fusion.4
  1988.3 1.8 convolution_add_fusion.1
  1990.1 2.0 fusion.33
  1992.4 129.5 %all-reduce.36.cloned.1.call-done = f32[512,512]{1,0:T(8,128)} async-done(((f32[512,512]{1,0:T(8,128)}), f32[512,512]{1,0:T(8,128)}) %all-reduce.36.cloned.1.call-update) | async-done | bytes 1048592 | tf_op jit(solution)/shard_map/psum | solution.py:19
  2122.0 3.8 fusion.3
  2125.8 2.5 fusion.25
  2129.5 2.0 fusion.34
  2131.6 24.0 all-gather.9.cloned.1.call-done
  2155.5 12.9 convolution_convert_fusion
  2168.4 61.2 %all-gather.11.cloned.1.call-done = bf16[512,3584]{1,0:T(8,128)(2,1)} async-done(((bf16[128,3584]{1,0:T(8,128)(2,1)}), bf16[512,3584]{1,0:T(8,128)(2,1)}) %all-gather.11.cloned.1.call-update) | async-done | bytes 3670032 | tf_op jit(solution)/shard_map/all_gather | solution.py:62
  2229.7 135.1 %all-reduce.38.cloned.1.call-done = f32[512,512]{1,0:T(8,128)} async-done(((f32[512,512]{1,0:T(8,128)}), f32[512,512]{1,0:T(8,128)}) %all-reduce.38.cloned.1.call-update) | async-done | bytes 1048592 | tf_op jit(solution)/shard_map/psum | solution.py:57
  2364.7 5.0 fusion.18
  2369.7 64.7 %reduce-scatter.8.cloned.1.call-done = bf16[128,3584]{1,0:T(8,128)(2,1)} async-done(((bf16[512,3584]{1,0:T(8,128)(2,1)}), bf16[128,3584]{1,0:T(8,128)(2,1)}) %reduce-scatter.8.cloned.1.call-update) | async-done | bytes 917520 | tf_op jit(solution)/shard_map/reduce_scatter | solution.py:49
  2434.4 2.6 convert_element_type.63
  (52 shorter events, 6.3 us)
Async XLA Ops:
  30.2 5.7 copy-start
  30.2 176.3 %all-to-all-start = ((bf16[256,8,3584]{0,2,1:T(8,128)(2,1)}), bf16[256,8,3584]{0,2,1:T(8,128)(2,1)}, u32[]{:S(2)}, u32[]{:S(2)}) async-start(bf16[256,8,3584]{0,2,1:T(8,128)(2,1)} %bitcast.76), calls=%async_computation | async-start | bytes 29360128 | tf_op jit(solution)/shard_map/all_to_all | solution.py:27
  35.9 189.4 %all-gather.5.cloned.1.call-start = ((), (), s32[]{:S(2)}) async-start(), calls=%async_computation.4 | async-start | bytes 2359296 | tf_op jit(solution)/shard_map/all_gather | solution.py:35
  36.7 339.9 %all-reduce.14.cloned.1.call-start = ((), (), s32[]{:S(2)}) async-start(), calls=%async_computation.5 | async-start | bytes 7340032 | tf_op jit(solution)/shard_map/psum | solution.py:39
  238.2 191.8 %reduce-scatter.4.cloned.1.call-start = ((), (), s32[]{:S(2)}) async-start(), calls=%async_computation.6 | async-start | bytes 2359296 | tf_op jit(solution)/shard_map/reduce_scatter | solution.py:40
  389.8 217.1 %all-reduce.16.cloned.1.call-start = ((), (), s32[]{:S(2)}) async-start(), calls=%async_computation.7 | async-start | bytes 2097152 | tf_op jit(solution)/shard_map/psum | solution.py:19
  430.1 180.7 %copy-start.2 = (bf16[256,512]{0,1:T(8,128)(2,1)S(1)}, bf16[256,512]{0,1:T(8,128)(2,1)}, u32[]{:S(2)}) copy-start(bf16[256,512]{0,1:T(8,128)(2,1)} %reduce-scatter.4.cloned.1.call-done) | copy-start | bytes 786436
  475.2 269.3 %all-reduce.18.cloned.1.call-start = ((), (), s32[]{:S(2)}) async-start(), calls=%async_computation.8 | async-start | bytes 2097152 | tf_op jit(solution)/shard_map/psum | solution.py:19
  614.6 267.3 %all-reduce.20.cloned.1.call-start = ((), (), s32[]{:S(2)}) async-start(), calls=%async_computation.9 | async-start | bytes 2097152 | tf_op jit(solution)/shard_map/psum | solution.py:19
  752.1 267.3 %all-reduce.22.cloned.1.call-start = ((), (), s32[]{:S(2)}) async-start(), calls=%async_computation.10 | async-start | bytes 2097152 | tf_op jit(solution)/shard_map/psum | solution.py:19
  889.6 267.3 %all-reduce.24.cloned.1.call-start = ((), (), s32[]{:S(2)}) async-start(), calls=%async_computation.11 | async-start | bytes 2097152 | tf_op jit(solution)/shard_map/psum | solution.py:19
  1027.1 163.4 %all-gather.7.cloned.1.call-start = ((), (), s32[]{:S(2)}) async-start(), calls=%async_computation.12 | async-start | bytes 2359296 | tf_op jit(solution)/shard_map/all_gather | solution.py:35
  1163.3 178.3 %all-reduce.26.cloned.1.call-start = ((), (), s32[]{:S(2)}) async-start(), calls=%async_computation.13 | async-start | bytes 7340032 | tf_op jit(solution)/shard_map/psum | solution.py:39
  1203.4 191.6 %reduce-scatter.6.cloned.1.call-start = ((), (), s32[]{:S(2)}) async-start(), calls=%async_computation.14 | async-start | bytes 2359296 | tf_op jit(solution)/shard_map/reduce_scatter | solution.py:40
  1354.8 217.2 %all-reduce.28.cloned.1.call-start = ((), (), s32[]{:S(2)}) async-start(), calls=%async_computation.15 | async-start | bytes 2097152 | tf_op jit(solution)/shard_map/psum | solution.py:19
  1395.1 180.7 %copy-start.3 = (bf16[256,512]{0,1:T(8,128)(2,1)S(1)}, bf16[256,512]{0,1:T(8,128)(2,1)}, u32[]{:S(2)}) copy-start(bf16[256,512]{0,1:T(8,128)(2,1)} %reduce-scatter.6.cloned.1.call-done) | copy-start | bytes 786436
  1440.2 269.3 %all-reduce.30.cloned.1.call-start = ((), (), s32[]{:S(2)}) async-start(), calls=%async_computation.16 | async-start | bytes 2097152 | tf_op jit(solution)/shard_map/psum | solution.py:19
  1579.7 267.3 %all-reduce.32.cloned.1.call-start = ((), (), s32[]{:S(2)}) async-start(), calls=%async_computation.17 | async-start | bytes 2097152 | tf_op jit(solution)/shard_map/psum | solution.py:19
  1717.2 267.3 %all-reduce.34.cloned.1.call-start = ((), (), s32[]{:S(2)}) async-start(), calls=%async_computation.18 | async-start | bytes 2097152 | tf_op jit(solution)/shard_map/psum | solution.py:19
  1854.7 267.3 %all-reduce.36.cloned.1.call-start = ((), (), s32[]{:S(2)}) async-start(), calls=%async_computation.19 | async-start | bytes 2097152 | tf_op jit(solution)/shard_map/psum | solution.py:19
  1992.2 136.2 %copy-start.1 = (f32[128,3584]{1,0:T(8,128)S(1)}, f32[128,3584]{1,0:T(8,128)}, u32[]{:S(2)}) copy-start(f32[128,3584]{1,0:T(8,128)} %param.5) | copy-start | bytes 5505028
  1992.2 163.4 %all-gather.9.cloned.1.call-start = ((), (), s32[]{:S(2)}) async-start(), calls=%async_computation.20 | async-start | bytes 2359296 | tf_op jit(solution)/shard_map/all_gather | solution.py:47
  2128.3 101.3 %all-gather.11.cloned.1.call-start = ((), (), s32[]{:S(2)}) async-start(), calls=%async_computation.23 | async-start | bytes 4587520 | tf_op jit(solution)/shard_map/all_gather | solution.py:62
  2129.4 235.3 %all-reduce.38.cloned.1.call-start = ((), (), s32[]{:S(2)}) async-start(), calls=%async_computation.22 | async-start | bytes 2097152 | tf_op jit(solution)/shard_map/psum | solution.py:57
  2131.5 302.9 %reduce-scatter.8.cloned.1.call-start = ((), (), s32[]{:S(2)}) async-start(), calls=%async_computation.21 | async-start | bytes 4587520 | tf_op jit(solution)/shard_map/reduce_scatter | solution.py:49
Sparse Core Ops, SparseCore 0:
  39.1 95.7 all-gather.4
  238.4 138.1 all-reduce.13
  389.9 40.1 reduce-scatter.3
  475.3 131.5 all-reduce.15
  614.8 129.6 all-reduce.17
  752.2 129.6 all-reduce.19
  889.8 129.6 all-reduce.21
  1027.3 129.6 all-reduce.23
  1163.5 27.0 all-gather.6
  1203.6 138.0 all-reduce.25
  1354.9 40.1 reduce-scatter.5
  1440.3 131.6 all-reduce.27
  1579.8 129.6 all-reduce.29
  1717.3 129.6 all-reduce.31
  1854.8 129.6 all-reduce.33
  1992.3 129.6 all-reduce.35
  2128.5 27.0 all-gather.8
  2157.5 72.0 all-gather.10
  2235.4 129.2 all-reduce.37
  2366.9 67.4 reduce-scatter.7
where the time goes:
time: 2450 us; the launch traced here: 2440 us
  waiting for transfers between devices  2140 us (87%)
  matrix products  152 us (6%)
  blocking collectives  79 us (3%)
  local copies, waits for them, and re-layouts  41.8 us (2%)
    psum x10, waiting for transfers between devices, orthogonal_sharded(): gram = lax.psum(jnp.dot(ortho.T, ortho, precision=highest), ('fsdp', 'col'))  1300 us
    psum x2, waiting for transfers between devices, local(): coeff = lax.psum(partial_coeff.astype(jnp.bfloat16), 'fsdp')  276 us
    all_to_all x1, waiting for transfers between devices, local(): lax.all_to_all(grad.astype(jnp.bfloat16), 'col', split_axis=1, concat_axi...  170 us
    psum x1, waiting for transfers between devices, local(): lax.psum(jnp.dot(basis.T, basis_old, precision=highest), ('fsdp', 'col'))  135 us
    reduce_scatter x2, waiting for transfers between devices, local(): lax.psum_scatter(jnp.dot(grad_tile, coeff, preferred_element_type=jnp.flo...  80.5 us
    psum x2, blocking collectives, orthogonal_sharded(): scale = lax.psum(jnp.sum(image * image), ('fsdp', 'col'))  79 us
    reduce_scatter x1, waiting for transfers between devices, local(): lax.psum_scatter(lax.dot_general(gathered, grad_tile, (((0,), (0,)), ((),...  64.7 us
    all_gather x1, waiting for transfers between devices, local(): lax.all_gather(moment.astype(jnp.bfloat16), 'fsdp', axis=0, tiled=True)  61.2 us
  transfers between devices with their start and end apart: 21, of which 20 were waited for; matrix products, arithmetic and copies ran while one was open for 2% of the time, Pallas kernels for 0%

commit v1 on v0

--- a/solution.py
+++ b/solution.py
@@ -36,7 +36,7 @@
             (((0,), (0,)), ((), ())),
             preferred_element_type=jnp.float32,
         )
-        coeff = lax.psum(partial_coeff.astype(jnp.bfloat16), "fsdp")
+        coeff = jnp.sum(lax.all_gather(partial_coeff.astype(jnp.bfloat16), "fsdp"), axis=0)
         image = lax.psum_scatter(
             jnp.dot(grad_tile, coeff, preferred_element_type=jnp.float32).astype(jnp.bfloat16),
             "col",

time: 2450 us -> 2740 us (1.12)
  waiting for transfers between devices: 2140 us -> 2370 us
  other arithmetic: 7.86 us -> 43.3 us
  local copies, waits for them, and re-layouts: 41.8 us -> 69.5 us
    all_gather x0 -> x2, waiting for transfers between devices: none -> 505 us  [local(): lax.all_gather(partial_coeff.astype(jnp.bfloat16), 'fsdp')]
    psum x2 -> x0, waiting for transfers between devices: 276 us -> none  [local(): coeff = lax.psum(partial_coeff.astype(jnp.bfloat16), 'fsdp')]
    reduce_sum x0 -> x2, other arithmetic: none -> 35.5 us  [local(): jnp.sum(lax.all_gather(partial_coeff.astype(jnp.bfloat16), 'fsdp'), axis=0)]
    all_gather x0 -> x1, local copies, waits for them, and re-layouts: none -> 27.6 us  [local(): lax.all_gather(partial_coeff.astype(jnp.bfloat16), 'fsdp')]
  transfers between devices with their start and end apart: 21 -> 21, of which waited for: 20 -> 20; matrix products, arithmetic and copies ran while one was open for 2% -> 1% of each run, Pallas kernels for 0% -> 0%
where the time goes in v1:
time: 2740 us; the launch traced here: 2730 us
  waiting for transfers between devices  2370 us (86%)
  matrix products  152 us (6%)
  blocking collectives  79.4 us (3%)
  local copies, waits for them, and re-layouts  69.5 us (3%)
  other arithmetic  43.3 us (2%)
    psum x10, waiting for transfers between devices, orthogonal_sharded(): gram = lax.psum(jnp.dot(ortho.T, ortho, precision=highest), ('fsdp', 'col'))  1300 us
    all_gather x2, waiting for transfers between devices, local(): lax.all_gather(partial_coeff.astype(jnp.bfloat16), 'fsdp')  505 us
    all_to_all x1, waiting for transfers between devices, local(): lax.all_to_all(grad.astype(jnp.bfloat16), 'col', split_axis=1, concat_axi...  170 us
    psum x1, waiting for transfers between devices, local(): lax.psum(jnp.dot(basis.T, basis_old, precision=highest), ('fsdp', 'col'))  135 us
    psum x2, blocking collectives, orthogonal_sharded(): scale = lax.psum(jnp.sum(image * image), ('fsdp', 'col'))  79.4 us
    reduce_scatter x2, waiting for transfers between devices, local(): lax.psum_scatter(jnp.dot(grad_tile, coeff, preferred_element_type=jnp.flo...  78.8 us
    reduce_scatter x1, waiting for transfers between devices, local(): lax.psum_scatter(lax.dot_general(gathered, grad_tile, (((0,), (0,)), ((),...  64.7 us
    all_gather x1, waiting for transfers between devices, local(): lax.all_gather(moment.astype(jnp.bfloat16), 'fsdp', axis=0, tiled=True)  61.2 us
  transfers between devices with their start and end apart: 21, of which 20 were waited for; matrix products, arithmetic and copies ran while one was open for 1% of the time, Pallas kernels for 0%

profile of v1, /device:TPU:0, one launch (start us, length us, event | category | flops | bytes accessed | tf_op | source)
XLA Modules:
  0.0 2734.6 jit_solution(17935298463080463558)
XLA Ops:
  7.2 23.0 copy.35
  30.2 5.7 all-to-all-start
  36.7 169.7 %all-to-all-done = bf16[256,8,3584]{0,2,1:T(8,128)(2,1)} async-done(((bf16[256,8,3584]{0,2,1:T(8,128)(2,1)}), bf16[256,8,3584]{0,2,1:T(8,128)(2,1)}, u32[]{:S(2)}, u32[]{:S(2)}) %all-to-all-start) | async-done | bytes 14680096 | tf_op jit(solution)/shard_map/all_to_all | solution.py:27
  206.5 18.8 copy.36
  225.2 12.9 convolution_convert_fusion.2
  238.3 252.7 %all-gather.17.cloned.1.call-done = bf16[14336,512]{1,0:T(8,128)(2,1)} async-done(((bf16[3584,512]{1,0:T(8,128)(2,1)}), bf16[14336,512]{1,0:T(8,128)(2,1)}) %all-gather.17.cloned.1.call-update) | async-done | bytes 14680080 | tf_op jit(solution)/shard_map/all_gather | solution.py:39
  491.0 10.7 reduce_sum.42
  501.6 13.2 fusion.1
  514.9 39.4 %reduce-scatter.4.cloned.1.call-done = bf16[256,512]{0,1:T(8,128)(2,1)} async-done(((bf16[2048,512]{0,1:T(8,128)(2,1)}), bf16[256,512]{0,1:T(8,128)(2,1)}) %reduce-scatter.4.cloned.1.call-update) | async-done | bytes 262160 | tf_op jit(solution)/shard_map/reduce_scatter | solution.py:40
  556.1 39.9 %psum.91 = f32[]{:T(128)} all-reduce(f32[]{:T(128)} %fusion.14), channel_id=1, replica_groups=mesh['fsdp'=4,'col'=8] {'fsdp','col'}, use_global_device_ids=true, to_apply=%region_3.0 | all-reduce | flops 1 | bytes 8 | tf_op jit(solution)/shard_map/psum | solution.py:16
  596.7 3.1 fusion.16
  599.8 131.7 %all-reduce.12.cloned.1.call-done = f32[512,512]{1,0:T(8,128)} async-done(((f32[512,512]{1,0:T(8,128)}), f32[512,512]{1,0:T(8,128)}) %all-reduce.12.cloned.1.call-update) | async-done | bytes 1048592 | tf_op jit(solution)/shard_map/psum | solution.py:19
  731.5 3.8 fusion.12
  737.2 2.0 fusion.26
  739.3 129.7 %all-reduce.14.cloned.1.call-done = f32[512,512]{1,0:T(8,128)} async-done(((f32[512,512]{1,0:T(8,128)}), f32[512,512]{1,0:T(8,128)}) %all-reduce.14.cloned.1.call-update) | async-done | bytes 1048592 | tf_op jit(solution)/shard_map/psum | solution.py:19
  869.0 3.8 fusion.11
  872.8 1.8 convolution_add_fusion.8
  874.7 2.0 fusion.27
  876.9 129.6 %all-reduce.16.cloned.1.call-done = f32[512,512]{1,0:T(8,128)} async-done(((f32[512,512]{1,0:T(8,128)}), f32[512,512]{1,0:T(8,128)}) %all-reduce.16.cloned.1.call-update) | async-done | bytes 1048592 | tf_op jit(solution)/shard_map/psum | solution.py:19
  1006.5 3.8 fusion.10
  1010.4 1.8 convolution_add_fusion.7
  1012.2 2.0 fusion.28
  1014.3 129.7 %all-reduce.18.cloned.1.call-done = f32[512,512]{1,0:T(8,128)} async-done(((f32[512,512]{1,0:T(8,128)}), f32[512,512]{1,0:T(8,128)}) %all-reduce.18.cloned.1.call-update) | async-done | bytes 1048592 | tf_op jit(solution)/shard_map/psum | solution.py:19
  1144.0 3.8 fusion.9
  1147.9 1.8 convolution_add_fusion.6
  1149.7 2.0 fusion.29
  1152.0 129.5 %all-reduce.20.cloned.1.call-done = f32[512,512]{1,0:T(8,128)} async-done(((f32[512,512]{1,0:T(8,128)}), f32[512,512]{1,0:T(8,128)}) %all-reduce.20.cloned.1.call-update) | async-done | bytes 1048592 | tf_op jit(solution)/shard_map/psum | solution.py:19
  1281.5 3.8 fusion.8
  1285.3 2.5 fusion.13
  1287.9 27.2 all-gather.11.cloned.1.call-done
  1315.1 12.9 fusion
  1328.3 252.3 %all-gather.19.cloned.1.call-done = bf16[14336,512]{0,1:T(8,128)(2,1)} async-done(((bf16[3584,512]{0,1:T(8,128)(2,1)}), bf16[14336,512]{0,1:T(8,128)(2,1)}) %all-gather.19.cloned.1.call-update) | async-done | bytes 14680080 | tf_op jit(solution)/shard_map/all_gather | solution.py:39
  1580.6 27.6 %reshape.8 = bf16[4,3584,512]{1,0,2:T(4,128)(2,1)} reshape(bf16[14336,512]{0,1:T(8,128)(2,1)} %all-gather.19.cloned.1.call-done) | data formatting | bytes 29360128 | tf_op jit(solution)/shard_map/all_gather | solution.py:39
  1608.2 24.8 reduce_sum.44
  1633.1 13.2 fusion.2
  1646.3 39.4 %reduce-scatter.6.cloned.1.call-done = bf16[256,512]{0,1:T(8,128)(2,1)} async-done(((bf16[2048,512]{0,1:T(8,128)(2,1)}), bf16[256,512]{0,1:T(8,128)(2,1)}) %reduce-scatter.6.cloned.1.call-update) | async-done | bytes 262160 | tf_op jit(solution)/shard_map/reduce_scatter | solution.py:40
  1687.5 39.5 %psum.97 = f32[]{:T(128)} all-reduce(f32[]{:T(128)} %fusion.15), channel_id=1, replica_groups=mesh['fsdp'=4,'col'=8] {'fsdp','col'}, use_global_device_ids=true, to_apply=%region_12.0 | all-reduce | flops 1 | bytes 8 | tf_op jit(solution)/shard_map/psum | solution.py:16
  1727.6 3.1 fusion.17
  1731.3 131.3 %all-reduce.22.cloned.1.call-done = f32[512,512]{1,0:T(8,128)} async-done(((f32[512,512]{1,0:T(8,128)}), f32[512,512]{1,0:T(8,128)}) %all-reduce.22.cloned.1.call-update) | async-done | bytes 1048592 | tf_op jit(solution)/shard_map/psum | solution.py:19
  1862.6 3.8 fusion.7
  1868.3 2.0 fusion.30
  1870.4 129.7 %all-reduce.24.cloned.1.call-done = f32[512,512]{1,0:T(8,128)} async-done(((f32[512,512]{1,0:T(8,128)}), f32[512,512]{1,0:T(8,128)}) %all-reduce.24.cloned.1.call-update) | async-done | bytes 1048592 | tf_op jit(solution)/shard_map/psum | solution.py:19
  2000.1 3.8 fusion.6
  2003.9 1.8 convolution_add_fusion.3
  2005.8 2.0 fusion.31
  2008.0 129.6 %all-reduce.26.cloned.1.call-done = f32[512,512]{1,0:T(8,128)} async-done(((f32[512,512]{1,0:T(8,128)}), f32[512,512]{1,0:T(8,128)}) %all-reduce.26.cloned.1.call-update) | async-done | bytes 1048592 | tf_op jit(solution)/shard_map/psum | solution.py:19
  2137.6 3.8 fusion.5
  2141.4 1.8 convolution_add_fusion.2
  2143.3 2.0 fusion.32
  2145.3 129.7 %all-reduce.28.cloned.1.call-done = f32[512,512]{1,0:T(8,128)} async-done(((f32[512,512]{1,0:T(8,128)}), f32[512,512]{1,0:T(8,128)}) %all-reduce.28.cloned.1.call-update) | async-done | bytes 1048592 | tf_op jit(solution)/shard_map/psum | solution.py:19
  2275.1 3.8 fusion.4
  2278.9 1.8 convolution_add_fusion.1
  2280.8 2.0 fusion.33
  2283.1 129.5 %all-reduce.30.cloned.1.call-done = f32[512,512]{1,0:T(8,128)} async-done(((f32[512,512]{1,0:T(8,128)}), f32[512,512]{1,0:T(8,128)}) %all-reduce.30.cloned.1.call-update) | async-done | bytes 1048592 | tf_op jit(solution)/shard_map/psum | solution.py:19
  2412.6 3.8 fusion.3
  2416.4 2.5 fusion.25
  2420.1 2.0 fusion.34
  2422.2 24.0 all-gather.13.cloned.1.call-done
  2446.2 12.9 convolution_convert_fusion
  2459.1 61.2 %all-gather.15.cloned.1.call-done = bf16[512,3584]{1,0:T(8,128)(2,1)} async-done(((bf16[128,3584]{1,0:T(8,128)(2,1)}), bf16[512,3584]{1,0:T(8,128)(2,1)}) %all-gather.15.cloned.1.call-update) | async-done | bytes 3670032 | tf_op jit(solution)/shard_map/all_gather | solution.py:62
  2520.3 135.0 %all-reduce.32.cloned.1.call-done = f32[512,512]{1,0:T(8,128)} async-done(((f32[512,512]{1,0:T(8,128)}), f32[512,512]{1,0:T(8,128)}) %all-reduce.32.cloned.1.call-update) | async-done | bytes 1048592 | tf_op jit(solution)/shard_map/psum | solution.py:57
  2655.3 5.0 fusion.18
  2660.2 64.7 %reduce-scatter.8.cloned.1.call-done = bf16[128,3584]{1,0:T(8,128)(2,1)} async-done(((bf16[512,3584]{1,0:T(8,128)(2,1)}), bf16[128,3584]{1,0:T(8,128)(2,1)}) %reduce-scatter.8.cloned.1.call-update) | async-done | bytes 917520 | tf_op jit(solution)/shard_map/reduce_scatter | solution.py:49
  2724.9 2.6 convert_element_type.67
  (55 shorter events, 11.6 us)
Async XLA Ops:
  30.2 5.7 copy-start
  30.2 176.3 %all-to-all-start = ((bf16[256,8,3584]{0,2,1:T(8,128)(2,1)}), bf16[256,8,3584]{0,2,1:T(8,128)(2,1)}, u32[]{:S(2)}, u32[]{:S(2)}) async-start(bf16[256,8,3584]{0,2,1:T(8,128)(2,1)} %bitcast.79), calls=%async_computation | async-start | bytes 29360128 | tf_op jit(solution)/shard_map/all_to_all | solution.py:27
  35.9 189.4 %all-gather.9.cloned.1.call-start = ((), (), s32[]{:S(2)}) async-start(), calls=%async_computation.4 | async-start | bytes 2359296 | tf_op jit(solution)/shard_map/all_gather | solution.py:35
  36.7 454.3 %all-gather.17.cloned.1.call-start = ((), (), s32[]{:S(2)}) async-start(), calls=%async_computation.22 | async-start | bytes 18350080 | tf_op jit(solution)/shard_map/all_gather | solution.py:39
  238.2 316.1 %reduce-scatter.4.cloned.1.call-start = ((), (), s32[]{:S(2)}) async-start(), calls=%async_computation.5 | async-start | bytes 2359296 | tf_op jit(solution)/shard_map/reduce_scatter | solution.py:40
  514.8 216.7 %all-reduce.12.cloned.1.call-start = ((), (), s32[]{:S(2)}) async-start(), calls=%async_computation.6 | async-start | bytes 2097152 | tf_op jit(solution)/shard_map/psum | solution.py:19
  554.3 181.1 %copy-start.2 = (bf16[256,512]{0,1:T(8,128)(2,1)S(1)}, bf16[256,512]{0,1:T(8,128)(2,1)}, u32[]{:S(2)}) copy-start(bf16[256,512]{0,1:T(8,128)(2,1)} %reduce-scatter.4.cloned.1.call-done) | copy-start | bytes 786436
  599.8 269.2 %all-reduce.14.cloned.1.call-start = ((), (), s32[]{:S(2)}) async-start(), calls=%async_computation.7 | async-start | bytes 2097152 | tf_op jit(solution)/shard_map/psum | solution.py:19
  739.2 267.3 %all-reduce.16.cloned.1.call-start = ((), (), s32[]{:S(2)}) async-start(), calls=%async_computation.8 | async-start | bytes 2097152 | tf_op jit(solution)/shard_map/psum | solution.py:19
  876.7 267.3 %all-reduce.18.cloned.1.call-start = ((), (), s32[]{:S(2)}) async-start(), calls=%async_computation.9 | async-start | bytes 2097152 | tf_op jit(solution)/shard_map/psum | solution.py:19
  1014.2 267.3 %all-reduce.20.cloned.1.call-start = ((), (), s32[]{:S(2)}) async-start(), calls=%async_computation.10 | async-start | bytes 2097152 | tf_op jit(solution)/shard_map/psum | solution.py:19
  1151.7 163.4 %all-gather.11.cloned.1.call-start = ((), (), s32[]{:S(2)}) async-start(), calls=%async_computation.11 | async-start | bytes 2359296 | tf_op jit(solution)/shard_map/all_gather | solution.py:35
  1287.9 292.7 %all-gather.19.cloned.1.call-start = ((), (), s32[]{:S(2)}) async-start(), calls=%async_computation.23 | async-start | bytes 18350080 | tf_op jit(solution)/shard_map/all_gather | solution.py:39
  1328.0 357.7 %reduce-scatter.6.cloned.1.call-start = ((), (), s32[]{:S(2)}) async-start(), calls=%async_computation.12 | async-start | bytes 2359296 | tf_op jit(solution)/shard_map/reduce_scatter | solution.py:40
  1646.2 216.4 %all-reduce.22.cloned.1.call-start = ((), (), s32[]{:S(2)}) async-start(), calls=%async_computation.13 | async-start | bytes 2097152 | tf_op jit(solution)/shard_map/psum | solution.py:19
  1685.7 180.7 %copy-start.3 = (bf16[256,512]{0,1:T(8,128)(2,1)S(1)}, bf16[256,512]{0,1:T(8,128)(2,1)}, u32[]{:S(2)}) copy-start(bf16[256,512]{0,1:T(8,128)(2,1)} %reduce-scatter.6.cloned.1.call-done) | copy-start | bytes 786436
  1730.8 269.3 %all-reduce.24.cloned.1.call-start = ((), (), s32[]{:S(2)}) async-start(), calls=%async_computation.14 | async-start | bytes 2097152 | tf_op jit(solution)/shard_map/psum | solution.py:19
  1870.3 267.3 %all-reduce.26.cloned.1.call-start = ((), (), s32[]{:S(2)}) async-start(), calls=%async_computation.15 | async-start | bytes 2097152 | tf_op jit(solution)/shard_map/psum | solution.py:19
  2007.8 267.3 %all-reduce.28.cloned.1.call-start = ((), (), s32[]{:S(2)}) async-start(), calls=%async_computation.16 | async-start | bytes 2097152 | tf_op jit(solution)/shard_map/psum | solution.py:19
  2145.3 267.3 %all-reduce.30.cloned.1.call-start = ((), (), s32[]{:S(2)}) async-start(), calls=%async_computation.17 | async-start | bytes 2097152 | tf_op jit(solution)/shard_map/psum | solution.py:19
  2282.8 136.2 %copy-start.1 = (f32[128,3584]{1,0:T(8,128)S(1)}, f32[128,3584]{1,0:T(8,128)}, u32[]{:S(2)}) copy-start(f32[128,3584]{1,0:T(8,128)} %param.5) | copy-start | bytes 5505028
  2282.8 163.4 %all-gather.13.cloned.1.call-start = ((), (), s32[]{:S(2)}) async-start(), calls=%async_computation.18 | async-start | bytes 2359296 | tf_op jit(solution)/shard_map/all_gather | solution.py:47
  2419.0 101.3 %all-gather.15.cloned.1.call-start = ((), (), s32[]{:S(2)}) async-start(), calls=%async_computation.21 | async-start | bytes 4587520 | tf_op jit(solution)/shard_map/all_gather | solution.py:62
  2420.1 235.2 %all-reduce.32.cloned.1.call-start = ((), (), s32[]{:S(2)}) async-start(), calls=%async_computation.20 | async-start | bytes 2097152 | tf_op jit(solution)/shard_map/psum | solution.py:57
  2422.1 302.8 %reduce-scatter.8.cloned.1.call-start = ((), (), s32[]{:S(2)}) async-start(), calls=%async_computation.19 | async-start | bytes 4587520 | tf_op jit(solution)/shard_map/reduce_scatter | solution.py:49
Sparse Core Ops, SparseCore 0:
  39.1 95.7 all-gather.8
  238.3 252.6 all-gather.16
  514.9 39.2 reduce-scatter.3
  599.9 131.5 all-reduce.11
  739.3 129.6 all-reduce.13
  876.8 129.6 all-reduce.15
  1014.3 129.6 all-reduce.17
  1151.8 129.6 all-reduce.19
  1288.0 27.0 all-gather.10
  1328.1 252.4 all-gather.18
  1646.4 39.2 reduce-scatter.5
  1730.9 131.6 all-reduce.21
  1870.4 129.6 all-reduce.23
  2007.9 129.6 all-reduce.25
  2145.4 129.6 all-reduce.27
  2282.9 129.6 all-reduce.29
  2419.1 27.0 all-gather.12
  2448.2 72.0 all-gather.14
  2526.0 129.1 all-reduce.31
  2657.4 67.4 reduce-scatter.7
